TPU v7x, 32 devices: a whole 2x2x4 slice. The times are simulated.
32 devices in a mesh: pb: 16 (over z, x, core), wa: 2 (over y).
Axes of the slice: x: 2, y: 2, z: 4, core: 2. Of those that a mesh axis runs over, the one named last changes fastest.
Arguments:
- psi_val: bfloat16 [16, 8, 1024], P('wa', None, 'pb'), may hold values from -0.796875 to 0.796875
- psi_cond: bfloat16 [16, 12, 1024], P('wa', None, 'pb'), may hold values from -0.796875 to 0.796875
- trials: bfloat16 [16, 1536], P('wa', 'pb'), may hold values from -6 to 6
- screened: bfloat16 [16, 1024, 1024], P('pb', 'wa'), may hold values from -0.1875 to 0.1875
- kmap: int32 [16, 16], P('pb'), may hold values from 0 to 15, each once within a row
Outputs:
- action: float32 [16, 1536], P('wa', 'pb')
Inputs may be any that keep to these rules, and one draw needn't show every extreme that they name: Every row of kmap is a permutation of the 16 k-points.
All inputs are finite; a program needn't handle non-finite values.
Results may differ from a plain program's by a relative error of at most 0.005.
Values may be sent and summed in bfloat16 or wider, within the bound.
A program may use at most 64 MiB of HBM per device.

v0:
```python
import math

import jax
import jax.numpy as jnp
from jax import lax
from jax.sharding import PartitionSpec as P


def shards(psi_val, psi_cond, trials, screened, kmap):
    hi = lax.Precision.HIGHEST
    wa_place = lax.axis_index("wa")
    val_part, cond_part, trial_part = (
        lax.all_gather(psi_val, "pb", axis=2, tiled=True),
        lax.all_gather(psi_cond, "pb", axis=2, tiled=True),
        lax.all_gather(trials, "pb", axis=1, tiled=True),
    )
    valence, conduct, xall = (
        lax.all_gather(val_part, "wa", axis=0, tiled=True),
        lax.all_gather(cond_part, "wa", axis=0, tiled=True),
        lax.all_gather(trial_part, "wa", axis=0, tiled=True),
    )
    kcount, nval, points = valence.shape
    ncond = conduct.shape[1]
    weights = screened[0]
    pairing = kmap[0]
    nrows = weights.shape[0]
    row_start = wa_place * nrows
    ntrial = xall.shape[1] // (nval * ncond)
    xfull = xall.astype(jnp.float32).reshape(kcount, ntrial, nval, ncond)
    val_pair = valence[pairing]
    cond_pair = conduct[pairing]
    x_pair = xfull[pairing]
    block = math.gcd(kcount, 2)
    contract = (((1,), (1,)), ((), ()))

    def one_block(index):
        start = index * block
        val_here = lax.dynamic_slice_in_dim(valence, start, block, 0).astype(jnp.float32)
        val_there = lax.dynamic_slice_in_dim(val_pair, start, block, 0).astype(jnp.float32)
        cond_here = lax.dynamic_slice_in_dim(conduct, start, block, 0).astype(jnp.float32)
        cond_there = lax.dynamic_slice_in_dim(cond_pair, start, block, 0).astype(jnp.float32)
        apair = (val_here[:, :, None, :] * val_there[:, None, :, :]).astype(jnp.bfloat16)
        bpair = (cond_here[:, :, None, :] * cond_there[:, None, :, :]).astype(jnp.bfloat16)
        apair = apair.reshape(block, nval * nval, points)
        bpair = bpair.reshape(block, ncond * ncond, points)
        wa_term = lax.dot_general(
            apair.reshape(-1, points), weights, contract, preferred_element_type=jnp.float32
        )
        wb_term = lax.dot_general(
            bpair.reshape(-1, points), weights, contract, preferred_element_type=jnp.float32
        )
        wa_term = wa_term.astype(jnp.bfloat16).reshape(block, nval * nval, nrows)
        wb_term = wb_term.astype(jnp.bfloat16).reshape(block, ncond * ncond, nrows)
        a_local = lax.dynamic_slice_in_dim(apair, row_start, nrows, 2)
        b_local = lax.dynamic_slice_in_dim(bpair, row_start, nrows, 2)
        gmat = jnp.einsum("kam,kbm->kab", wa_term, b_local, preferred_element_type=jnp.float32)
        hmat = jnp.einsum("kam,kbm->kab", a_local, wb_term, preferred_element_type=jnp.float32)
        gmat = gmat.reshape(block, nval, nval, ncond, ncond)
        hmat = hmat.reshape(block, nval, nval, ncond, ncond)
        x_there = lax.dynamic_slice_in_dim(x_pair, start, block, 0)
        x_here = lax.dynamic_slice_in_dim(xfull, start, block, 0)
        forward = jnp.einsum("kvucd,ksud->ksvc", gmat, x_there, precision=hi)
        backward = jnp.einsum("kuvdc,ksud->ksvc", hmat, x_here, precision=hi)
        return (forward, backward)

    forward, backward = lax.map(one_block, jnp.arange(kcount // block, dtype=jnp.int32))
    forward = forward.reshape(kcount, ntrial, nval, ncond)
    backward = backward.reshape(kcount, ntrial, nval, ncond)
    partial_value = forward + jnp.zeros_like(forward).at[pairing].add(backward)
    flat = partial_value.reshape(kcount, ntrial * nval * ncond)
    result = lax.psum_scatter(flat, "pb", scatter_dimension=1, tiled=True)
    result = lax.psum_scatter(result, "wa", scatter_dimension=0, tiled=True)
    return result


def solution(mesh):
    in_specs = (
        P("wa", None, "pb"),
        P("wa", None, "pb"),
        P("wa", "pb"),
        P("pb", "wa", None),
        P("pb", None),
    )
    out_specs = P("wa", "pb")
    return jax.shard_map(shards, mesh=mesh, in_specs=in_specs, out_specs=out_specs, check_vma=False)
```

profile of v0, /device:TPU:5, one launch (start us, length us, event | category | flops | bytes accessed | tf_op | source)
XLA Modules:
  0.0 302.9 jit_solution(9937651773412034785)
XLA Ops:
  6.5 22.4 %all-gather = bf16[16,96,8]{1,2,0:T(8,128)(2,1)S(1)} all-gather(bf16[1,96,8]{1,2,0:T(8,128)(2,1)} %bitcast.103), channel_id=1, replica_groups=mesh['pb'=16,'wa'=2] {'pb'}, dimensions={0}, use_global_device_ids=true | all-gather | bytes 26112 | tf_op jit(solution)/shard_map/all_gather | solution.py:15
  29.1 3.3 %all_gather.19 = bf16[16,1536]{1,0:T(8,128)(2,1)S(1)} all-gather(bf16[8,1536]{1,0:T(8,128)(2,1)S(1)} %bitcast.101), channel_id=1, replica_groups=mesh['pb'=16,'wa'=2] {'wa'}, dimensions={0}, use_global_device_ids=true | all-gather | bytes 73728 | tf_op jit(solution)/shard_map/all_gather | solution.py:20
  32.4 1.1 reshape.111
  35.1 30.7 %all_gather.20 = bf16[8,8,1024]{1,0,2:T(8,128)(2,1)S(1)} all-gather(bf16[8,8,64]{1,0,2:T(8,128)(2,1)S(1)} %copy.39), channel_id=1, replica_groups=mesh['pb'=16,'wa'=2] {'pb'}, dimensions={2}, use_global_device_ids=true | all-gather | bytes 139264 | tf_op jit(solution)/shard_map/all_gather | solution.py:13
  65.8 1.4 copy.40
  67.2 5.7 %all_gather.21 = bf16[16,8,1024]{2,1,0:T(8,128)(2,1)S(1)} all-gather(bf16[8,8,1024]{2,1,0:T(8,128)(2,1)S(1)} %copy.40), channel_id=1, replica_groups=mesh['pb'=16,'wa'=2] {'wa'}, dimensions={0}, use_global_device_ids=true | all-gather | bytes 393216 | tf_op jit(solution)/shard_map/all_gather | solution.py:18
  72.9 1.6 gather_fusion
  74.5 1.3 gather_fusion.1
  75.9 28.8 %all_gather.22 = bf16[8,12,1024]{1,0,2:T(8,128)(2,1)S(1)} all-gather(bf16[8,12,64]{1,0,2:T(8,128)(2,1)S(1)} %copy.41), channel_id=1, replica_groups=mesh['pb'=16,'wa'=2] {'pb'}, dimensions={2}, use_global_device_ids=true | all-gather | bytes 208896 | tf_op jit(solution)/shard_map/all_gather | solution.py:14
  104.7 2.2 copy.42
  106.8 7.5 %all_gather.23 = bf16[16,12,1024]{2,0,1:T(8,128)(2,1)S(1)} all-gather(bf16[8,12,1024]{2,0,1:T(8,128)(2,1)} %copy.42), channel_id=1, replica_groups=mesh['pb'=16,'wa'=2] {'wa'}, dimensions={0}, use_global_device_ids=true | all-gather | bytes 589824 | tf_op jit(solution)/shard_map/all_gather | solution.py:19
  114.3 1.0 copy.45
  115.3 2.4 gather_fusion.2
  117.8 113.2 %while.14 = (s32[]{:T(128)}, f32[8,2,16,8,12]{2,3,4,1,0:T(8,128)}, f32[8,2,16,8,12]{4,2,3,1,0:T(8,128)}, s32[8]{0:T(128)S(1)}, f32[16,16,8,12]{3,2,1,0:T(8,128)}...) while((s32[]{:T(128)}, f32[8,2,16,8,12]{2,3,4,1,0:T(8,128)}, ...), condition=%wide.region_1.2_spmd, body=%wide.region_0.1_spmd.sunk | while | flops 482181120 | bytes 12149035 | solution.py:66
  123.1 1.0 constant_dynamic-slice_fusion.7
  124.1 3.7 %convolution_bitcast_fusion.3 = f32[1,2,16,8,12]{4,2,3,1,0:T(8,128)S(1)} fusion(f32[2,8,8,12,12]{4,3,2,1,0:T(8,128)S(1)} %reshape.156, f32[2,16,8,12]{3,2,1,0:T(8,128)S(1)} %get-tuple-element.302), kind=kOutput, calls=%fused_computation.9.clone.1 | convolution fusion | flops 3538944 | bytes 98304 | tf_op jit(solution)/shard_map/while/body/eval_jaxpr/kvucd,ksud->ksvc/dot_general | solution.py:62
  130.1 1.9 fusion.47
  134.7 0.9 dynamic-slice_convert_fusion.7
  137.2 1.0 constant_dynamic-slice_fusion.7
  138.2 3.7 %convolution_bitcast_fusion.3 = f32[1,2,16,8,12]{4,2,3,1,0:T(8,128)S(1)} fusion(f32[2,8,8,12,12]{4,3,2,1,0:T(8,128)S(1)} %reshape.156, f32[2,16,8,12]{3,2,1,0:T(8,128)S(1)} %get-tuple-element.302), kind=kOutput, calls=%fused_computation.9.clone.1 | convolution fusion | flops 3538944 | bytes 98304 | tf_op jit(solution)/shard_map/while/body/eval_jaxpr/kvucd,ksud->ksvc/dot_general | solution.py:62
  144.2 1.9 fusion.47
  148.8 0.9 dynamic-slice_convert_fusion.7
  151.4 1.0 constant_dynamic-slice_fusion.7
  152.4 3.7 %convolution_bitcast_fusion.3 = f32[1,2,16,8,12]{4,2,3,1,0:T(8,128)S(1)} fusion(f32[2,8,8,12,12]{4,3,2,1,0:T(8,128)S(1)} %reshape.156, f32[2,16,8,12]{3,2,1,0:T(8,128)S(1)} %get-tuple-element.302), kind=kOutput, calls=%fused_computation.9.clone.1 | convolution fusion | flops 3538944 | bytes 98304 | tf_op jit(solution)/shard_map/while/body/eval_jaxpr/kvucd,ksud->ksvc/dot_general | solution.py:62
  158.3 1.9 fusion.47
  163.0 0.9 dynamic-slice_convert_fusion.7
  165.5 1.0 constant_dynamic-slice_fusion.7
  166.5 3.7 %convolution_bitcast_fusion.3 = f32[1,2,16,8,12]{4,2,3,1,0:T(8,128)S(1)} fusion(f32[2,8,8,12,12]{4,3,2,1,0:T(8,128)S(1)} %reshape.156, f32[2,16,8,12]{3,2,1,0:T(8,128)S(1)} %get-tuple-element.302), kind=kOutput, calls=%fused_computation.9.clone.1 | convolution fusion | flops 3538944 | bytes 98304 | tf_op jit(solution)/shard_map/while/body/eval_jaxpr/kvucd,ksud->ksvc/dot_general | solution.py:62
  172.5 1.9 fusion.47
  177.1 0.9 dynamic-slice_convert_fusion.7
  179.7 1.0 constant_dynamic-slice_fusion.7
  180.7 3.7 %convolution_bitcast_fusion.3 = f32[1,2,16,8,12]{4,2,3,1,0:T(8,128)S(1)} fusion(f32[2,8,8,12,12]{4,3,2,1,0:T(8,128)S(1)} %reshape.156, f32[2,16,8,12]{3,2,1,0:T(8,128)S(1)} %get-tuple-element.302), kind=kOutput, calls=%fused_computation.9.clone.1 | convolution fusion | flops 3538944 | bytes 98304 | tf_op jit(solution)/shard_map/while/body/eval_jaxpr/kvucd,ksud->ksvc/dot_general | solution.py:62
  186.6 1.9 fusion.47
  193.8 1.0 constant_dynamic-slice_fusion.7
  194.8 3.7 %convolution_bitcast_fusion.3 = f32[1,2,16,8,12]{4,2,3,1,0:T(8,128)S(1)} fusion(f32[2,8,8,12,12]{4,3,2,1,0:T(8,128)S(1)} %reshape.156, f32[2,16,8,12]{3,2,1,0:T(8,128)S(1)} %get-tuple-element.302), kind=kOutput, calls=%fused_computation.9.clone.1 | convolution fusion | flops 3538944 | bytes 98304 | tf_op jit(solution)/shard_map/while/body/eval_jaxpr/kvucd,ksud->ksvc/dot_general | solution.py:62
  200.8 1.9 fusion.47
  208.0 1.0 constant_dynamic-slice_fusion.7
  209.0 3.7 %convolution_bitcast_fusion.3 = f32[1,2,16,8,12]{4,2,3,1,0:T(8,128)S(1)} fusion(f32[2,8,8,12,12]{4,3,2,1,0:T(8,128)S(1)} %reshape.156, f32[2,16,8,12]{3,2,1,0:T(8,128)S(1)} %get-tuple-element.302), kind=kOutput, calls=%fused_computation.9.clone.1 | convolution fusion | flops 3538944 | bytes 98304 | tf_op jit(solution)/shard_map/while/body/eval_jaxpr/kvucd,ksud->ksvc/dot_general | solution.py:62
  214.9 1.9 fusion.47
  222.1 1.0 constant_dynamic-slice_fusion.7
  223.1 3.7 %convolution_bitcast_fusion.3 = f32[1,2,16,8,12]{4,2,3,1,0:T(8,128)S(1)} fusion(f32[2,8,8,12,12]{4,3,2,1,0:T(8,128)S(1)} %reshape.156, f32[2,16,8,12]{3,2,1,0:T(8,128)S(1)} %get-tuple-element.302), kind=kOutput, calls=%fused_computation.9.clone.1 | convolution fusion | flops 3538944 | bytes 98304 | tf_op jit(solution)/shard_map/while/body/eval_jaxpr/kvucd,ksud->ksvc/dot_general | solution.py:62
  229.1 1.9 fusion.47
  230.9 2.1 copy.48
  233.1 1.5 scatter_fusion
  234.6 1.0 copy.56
  235.6 1.0 reshape.153
  237.8 52.9 %reduce-scatter.4.cloned.1.call-done = f32[96,16]{1,0:T(8,128)} async-done(((f32[1536,16]{1,0:T(8,128)}), f32[96,16]{1,0:T(8,128)}) %reduce-scatter.4.cloned.1.call-update) | async-done | bytes 6160
  291.6 3.8 %all-reduce = f32[16,96]{1,0:T(8,128)S(1)} all-reduce(f32[16,96]{1,0:T(8,128)S(1)} %copy.55), channel_id=3, replica_groups=mesh['pb'=16,'wa'=2] {'wa'}, use_global_device_ids=true, to_apply=%region_4.5.clone | all-reduce | flops 1536 | bytes 12288
  (180 shorter events, 54.1 us)
Async XLA Ops:
  6.5 284.2 %reduce-scatter.4.cloned.1.call-start = ((), (), s32[]{:S(2)}) async-start(), calls=%async_computation.1 | async-start | bytes 835584
  33.6 39.3 %copy-start.1 = (f32[16,16,8,12]{3,2,1,0:T(8,128)}, f32[16,16,8,12]{3,2,1,0:T(8,128)S(1)}, u32[]{:S(2)}) copy-start(f32[16,16,8,12]{3,2,1,0:T(8,128)S(1)} %reshape.111) | copy-start | bytes 294916
  67.2 8.6 %copy-start.5 = (bf16[8,12,64]{2,0,1:T(8,128)(2,1)S(1)}, bf16[8,12,64]{2,0,1:T(8,128)(2,1)}, u32[]{:S(2)}) copy-start(bf16[8,12,64]{2,0,1:T(8,128)(2,1)} %param.8) | copy-start | bytes 36868
  106.8 10.9 %copy-start = (bf16[1,512,1024]{2,1,0:T(8,128)(2,1)S(1)}, bf16[1,512,1024]{2,1,0:T(8,128)(2,1)}, u32[]{:S(2)}) copy-start(bf16[1,512,1024]{2,1,0:T(8,128)(2,1)} %param.10) | copy-start | bytes 3145732
  117.8 3.8 %copy-start.3 = (bf16[16,8,1024]{2,1,0:T(8,128)(2,1)}, bf16[16,8,1024]{2,1,0:T(8,128)(2,1)S(1)}, u32[]{:S(2)}) copy-start(bf16[16,8,1024]{2,1,0:T(8,128)(2,1)S(1)} %get-tuple-element.342) | copy-start | bytes 786436 | tf_op jit(solution)/shard_map/while
  129.3 2.6 copy-start.4
  131.9 3.8 %copy-start.3 = (bf16[16,8,1024]{2,1,0:T(8,128)(2,1)}, bf16[16,8,1024]{2,1,0:T(8,128)(2,1)S(1)}, u32[]{:S(2)}) copy-start(bf16[16,8,1024]{2,1,0:T(8,128)(2,1)S(1)} %get-tuple-element.342) | copy-start | bytes 786436 | tf_op jit(solution)/shard_map/while
  143.5 2.6 copy-start.4
  146.1 3.8 %copy-start.3 = (bf16[16,8,1024]{2,1,0:T(8,128)(2,1)}, bf16[16,8,1024]{2,1,0:T(8,128)(2,1)S(1)}, u32[]{:S(2)}) copy-start(bf16[16,8,1024]{2,1,0:T(8,128)(2,1)S(1)} %get-tuple-element.342) | copy-start | bytes 786436 | tf_op jit(solution)/shard_map/while
  157.6 2.6 copy-start.4
  160.2 3.8 %copy-start.3 = (bf16[16,8,1024]{2,1,0:T(8,128)(2,1)}, bf16[16,8,1024]{2,1,0:T(8,128)(2,1)S(1)}, u32[]{:S(2)}) copy-start(bf16[16,8,1024]{2,1,0:T(8,128)(2,1)S(1)} %get-tuple-element.342) | copy-start | bytes 786436 | tf_op jit(solution)/shard_map/while
  171.8 2.6 copy-start.4
  174.4 3.8 %copy-start.3 = (bf16[16,8,1024]{2,1,0:T(8,128)(2,1)}, bf16[16,8,1024]{2,1,0:T(8,128)(2,1)S(1)}, u32[]{:S(2)}) copy-start(bf16[16,8,1024]{2,1,0:T(8,128)(2,1)S(1)} %get-tuple-element.342) | copy-start | bytes 786436 | tf_op jit(solution)/shard_map/while
  185.9 2.6 copy-start.4
  188.5 3.8 %copy-start.3 = (bf16[16,8,1024]{2,1,0:T(8,128)(2,1)}, bf16[16,8,1024]{2,1,0:T(8,128)(2,1)S(1)}, u32[]{:S(2)}) copy-start(bf16[16,8,1024]{2,1,0:T(8,128)(2,1)S(1)} %get-tuple-element.342) | copy-start | bytes 786436 | tf_op jit(solution)/shard_map/while
  200.1 2.6 copy-start.4
  202.7 3.8 %copy-start.3 = (bf16[16,8,1024]{2,1,0:T(8,128)(2,1)}, bf16[16,8,1024]{2,1,0:T(8,128)(2,1)S(1)}, u32[]{:S(2)}) copy-start(bf16[16,8,1024]{2,1,0:T(8,128)(2,1)S(1)} %get-tuple-element.342) | copy-start | bytes 786436 | tf_op jit(solution)/shard_map/while
  214.2 2.6 copy-start.4
  216.8 3.8 %copy-start.3 = (bf16[16,8,1024]{2,1,0:T(8,128)(2,1)}, bf16[16,8,1024]{2,1,0:T(8,128)(2,1)S(1)}, u32[]{:S(2)}) copy-start(bf16[16,8,1024]{2,1,0:T(8,128)(2,1)S(1)} %get-tuple-element.342) | copy-start | bytes 786436 | tf_op jit(solution)/shard_map/while
  228.3 2.6 copy-start.4
  230.9 2.1 copy-start.2
  235.6 1.0 copy-start.6
Sparse Core Ops, SparseCore 0:
  236.7 53.9 reduce-scatter.3
where the time goes:
time: 309 us; the launch traced here: 303 us
  blocking collectives  102 us (33%)
  matrix products  56.3 us (18%)
  local copies, waits for them, and re-layouts  53.8 us (17%)
  waiting for transfers between devices  52.9 us (17%)
  other arithmetic  17.1 us (6%)
  between operations  14.1 us (5%)
  loops' own time  6.46 us (2%)
    unnamed x2, waiting for transfers between devices  52.9 us
    all_gather x1, blocking collectives, shards(): lax.all_gather(psi_val, 'pb', axis=2, tiled=True)  30.7 us
    dot_general x8, matrix products, one_block(): forward = jnp.einsum('kvucd,ksud->ksvc', gmat, x_there, precision=hi)  30 us
    all_gather x1, blocking collectives, shards(): lax.all_gather(psi_cond, 'pb', axis=2, tiled=True)  28.8 us
    all_gather x1, blocking collectives, shards(): lax.all_gather(trials, 'pb', axis=1, tiled=True)  22.4 us
    dot_general x8, matrix products, one_block(): backward = jnp.einsum('kuvdc,ksud->ksvc', hmat, x_here, precision=hi)  15 us
    dynamic_slice x8, local copies, waits for them, and re-layouts, one_block(): x_here = lax.dynamic_slice_in_dim(xfull, start, block, 0)  7.95 us
    all_gather x1, blocking collectives, shards(): lax.all_gather(cond_part, 'wa', axis=0, tiled=True)  7.48 us
  transfers between devices with their start and end apart: 1, of which 1 were waited for; matrix products, arithmetic and copies ran while one was open for 0% of the time, Pallas kernels for 0%

commit v1 on v0

v1 whole, which is shorter than its diff:
```python
import functools
import math

import jax
import jax.numpy as jnp
from jax import lax
from jax.experimental import pallas as pl
from jax.experimental.pallas import tpu as pltpu
from jax.sharding import PartitionSpec as P

MESH = pl.DeviceIdType.MESH
LANES = 128
PACK = 16
F32 = jnp.float32
BF16 = jnp.bfloat16


def up(value, unit):
    return -(-value // unit) * unit


def gather_kernel(npb, nwa, x_ref, out_ref, own_sem, send_sem, recv_sem, fsend_sem, frecv_sem):
    pb, wa = lax.axis_index("pb"), lax.axis_index("wa")
    core = lax.rem(pb, 2)
    chip = (pb // 2) * nwa + wa
    nchips = npb // 2 * nwa

    def place(t, c):
        return (t // nwa) * 2 + c, lax.rem(t, nwa)

    barrier = pltpu.get_barrier_semaphore()
    pl.semaphore_signal(barrier, inc=1, device_id=place(chip, 1 - core), device_id_type=MESH)

    def greet(j, carry):
        t = lax.rem(chip + j, nchips)
        pl.semaphore_signal(barrier, inc=1, device_id=place(t, core), device_id_type=MESH)
        return carry

    lax.fori_loop(1, nchips, greet, 0)
    own = pltpu.make_async_copy(x_ref, out_ref.at[chip * 2 + core], own_sem)
    own.start()
    pl.semaphore_wait(barrier, nchips)

    def first(j):
        t = lax.rem(chip + j, nchips)
        return pltpu.make_async_remote_copy(
            src_ref=x_ref, dst_ref=out_ref.at[chip * 2 + core], send_sem=send_sem.at[j],
            recv_sem=recv_sem.at[j], device_id=place(t, core), device_id_type=MESH)

    def arrival(j):
        t = lax.rem(chip - j + nchips, nchips)
        return pltpu.make_async_remote_copy(
            src_ref=x_ref, dst_ref=out_ref.at[t * 2 + core], send_sem=send_sem.at[j],
            recv_sem=recv_sem.at[j], device_id=place(t, core), device_id_type=MESH)

    def second(j, source, c):
        t = lax.rem(chip - j + nchips, nchips)
        return pltpu.make_async_remote_copy(
            src_ref=source if source is not None else out_ref.at[t * 2 + core],
            dst_ref=out_ref.at[t * 2 + c], send_sem=fsend_sem.at[j],
            recv_sem=frecv_sem.at[j], device_id=place(chip, 1 - core), device_id_type=MESH)

    def send(j, carry):
        first(j).start()
        return carry

    lax.fori_loop(1, nchips, send, 0)
    second(0, x_ref, core).start()

    def forward(j, carry):
        arrival(j).wait_recv()
        second(j, None, core).start()
        return carry

    lax.fori_loop(1, nchips, forward, 0)

    def finish(j, carry):
        second(j, None, 1 - core).wait_recv()
        second(j, None, core).wait_send()
        return carry

    def finish_first(j, carry):
        first(j).wait_send()
        return carry

    lax.fori_loop(0, nchips, finish, 0)
    lax.fori_loop(1, nchips, finish_first, 0)
    own.wait()


def reduce_kernel(npb, nwa, x_ref, out_ref, slots, own_sem, send_sem, recv_sem):
    pb, wa = lax.axis_index("pb"), lax.axis_index("wa")
    me = pb * nwa + wa
    n = npb * nwa
    barrier = pltpu.get_barrier_semaphore()

    def place(t):
        return t // nwa, lax.rem(t, nwa)

    def greet(j, carry):
        pl.semaphore_signal(barrier, inc=1, device_id=place(lax.rem(me + j, n)), device_id_type=MESH)
        return carry

    lax.fori_loop(1, n, greet, 0)
    own = pltpu.make_async_copy(x_ref.at[me], slots.at[0], own_sem)
    own.start()
    pl.semaphore_wait(barrier, n - 1)

    def copy(j):
        t = lax.rem(me + j, n)
        return pltpu.make_async_remote_copy(
            src_ref=x_ref.at[t], dst_ref=slots.at[j], send_sem=send_sem.at[j],
            recv_sem=recv_sem.at[j], device_id=place(t), device_id_type=MESH)

    def send(j, carry):
        copy(j).start()
        return carry

    lax.fori_loop(1, n, send, 0)
    own.wait()

    def receive(j, carry):
        copy(j).wait_recv()
        return carry

    lax.fori_loop(1, n, receive, 0)
    total = slots[0]
    for j in range(1, n):
        total = total + slots[j]
    out_ref[...] = total

    def finish(j, carry):
        copy(j).wait_send()
        return carry

    lax.fori_loop(1, n, finish, 0)


def compute_kernel(dims, kmap_ref, inv_ref, val_ref, cond_ref, x_ref, w_ref, out_ref,
                   a_ref, wa_ref, aw_ref, y_ref, z_ref, acc_ref):
    kcount, nval, ncond, ntrial, points, nrows, nwa, npb = dims
    klocal = kcount // nwa
    crows = cond_ref.shape[1]
    row0 = pl.multiple_of(lax.axis_index("wa") * nrows, nrows)
    pairs = nval * nval
    block = math.gcd(kcount, max(1, 256 // pairs))

    def one_y(k, carry):
        y_ref[k] = lax.dot_general(x_ref[k], cond_ref[k], (((1,), (0,)), ((), ())), preferred_element_type=F32)
        return carry

    lax.fori_loop(0, kcount, one_y, 0)

    def build(b, index_ref, start, width):
        for i in range(block):
            k = b * block + i
            here = val_ref[k, :, pl.ds(start, width)]
            there = val_ref[index_ref[k], :, pl.ds(start, width)]
            for v in range(0, nval, 2):
                two = jnp.concatenate([here[v:v + 1] * there, here[v + 1:v + 2] * there], axis=0)
                a_ref[pl.ds(i * pairs + v * nval, 2 * nval), 0:width] = two.astype(BF16)

    def first(b, carry):
        build(b, kmap_ref, 0, points)
        out = lax.dot_general(a_ref[...], w_ref[...], (((1,), (1,)), ((), ())), preferred_element_type=F32)
        wa_ref[pl.ds(b * block, block)] = out.astype(BF16).astype(F32).reshape(block, pairs, nrows)
        return carry

    lax.fori_loop(0, kcount // block, first, 0)

    def second(b, carry):
        build(b, inv_ref, row0, nrows)
        out = lax.dot_general(a_ref[:, 0:nrows], w_ref[...], (((1,), (0,)), ((), ())), preferred_element_type=F32)
        aw_ref[pl.ds(b * block, block)] = out.reshape(block, pairs, points)
        return carry

    lax.fori_loop(0, kcount // block, second, 0)
    acc_ref[...] = jnp.zeros_like(acc_ref)
    chunk = math.gcd(nrows, LANES)

    def combine(k, weight_ref, other, start, base, width):
        for c in range(0, width, chunk):
            at = pl.ds(pl.multiple_of(start + c, chunk), chunk)
            ys = [y_ref[other, u * ntrial:(u + 1) * ntrial, at] for u in range(nval)]
            for v in range(nval):
                total = None
                for u in range(nval):
                    row = v * nval + u
                    term = weight_ref[k, row:row + 1, c:c + chunk] * ys[u]
                    total = term if total is None else total + term
                z_ref[v * ntrial:(v + 1) * ntrial, base + c:base + c + chunk] = total.astype(BF16)

    def one_k(k, carry):
        combine(k, wa_ref, kmap_ref[k], row0, 0, nrows)
        combine(k, aw_ref, inv_ref[k], 0, nrows, points)
        spot = lax.rem(k, klocal)
        both = jnp.concatenate([cond_ref[k, :, pl.ds(row0, nrows)], cond_ref[k]], axis=1)
        wide = jnp.concatenate(
            [both * jnp.where(spot == j, 1.0, 0.0).astype(BF16) for j in range(klocal)], axis=0)
        acc_ref[k // klocal] += lax.dot_general(
            z_ref[...], wide, (((1,), (1,)), ((), ())), preferred_element_type=F32)
        return carry

    lax.fori_loop(0, kcount, one_k, 0)
    r = out_ref.shape[1]
    for i in range(npb):
        s, v0 = i * r // nval, i * r % nval
        for w in range(nwa):
            out_ref[i * nwa + w] = acc_ref[w, pl.ds(v0 * ntrial + s, r, stride=ntrial), :]


def shards(npb, nwa, psi_val, psi_cond, trials, screened, kmap):
    klocal, nval, pts = psi_val.shape
    ncond = psi_cond.shape[1]
    cols = trials.shape[1]
    kcount, points = klocal * nwa, pts * npb
    ntrial = cols * npb // (nval * ncond)
    weights = screened[0]
    nrows = weights.shape[0]
    row = kmap[0]
    inverse = jnp.sum(
        jnp.where(row[None, :] == jnp.arange(kcount, dtype=jnp.int32)[:, None], jnp.arange(kcount, dtype=jnp.int32)[None, :], 0),
        axis=1).astype(jnp.int32)
    vmem = pl.BlockSpec(memory_space=pltpu.VMEM)
    smem = pl.BlockSpec(memory_space=pltpu.SMEM)

    flat = jnp.concatenate([psi_val.reshape(-1), psi_cond.reshape(-1), trials.reshape(-1)])
    size = flat.shape[0]
    rows = up(-(-size // LANES), PACK)
    packed = jnp.pad(flat, (0, rows * LANES - size)).reshape(rows, LANES)
    n = npb * nwa
    nchips = n // 2
    gathered = pl.pallas_call(
        functools.partial(gather_kernel, npb, nwa),
        out_shape=jax.ShapeDtypeStruct((n, rows, LANES), BF16),
        in_specs=[vmem], out_specs=vmem,
        scratch_shapes=[pltpu.SemaphoreType.DMA] + [pltpu.SemaphoreType.DMA((nchips,))] * 4,
        compiler_params=pltpu.CompilerParams(collective_id=0, has_side_effects=True),
        name="gather",
    )(packed)
    gathered = gathered.reshape(npb // 2, nwa, 2, rows * LANES)
    nv, nc = klocal * nval * pts, klocal * ncond * pts
    val = gathered[..., :nv].reshape(npb // 2, nwa, 2, klocal, nval, pts)
    cond = gathered[..., nv:nv + nc].reshape(npb // 2, nwa, 2, klocal, ncond, pts)
    tri = gathered[..., nv + nc:size].reshape(npb // 2, nwa, 2, klocal, cols)
    val = val.transpose(1, 3, 4, 0, 2, 5).reshape(kcount, nval, points).astype(F32)
    cond = cond.transpose(1, 3, 4, 0, 2, 5).reshape(kcount, ncond, points)
    crows = up(ncond, PACK)
    cond = jnp.pad(cond, ((0, 0), (0, crows - ncond), (0, 0)))
    tri = tri.transpose(1, 3, 0, 2, 4).reshape(kcount, ntrial, nval, ncond)
    tri = jnp.pad(tri.transpose(0, 2, 1, 3).reshape(kcount, nval * ntrial, ncond), ((0, 0), (0, 0), (0, crows - ncond)))

    r = cols // ncond
    width = klocal * crows
    pairs = nval * nval
    block = math.gcd(kcount, max(1, 256 // pairs))
    dims = (kcount, nval, ncond, ntrial, points, nrows, nwa, npb)
    partial = pl.pallas_call(
        functools.partial(compute_kernel, dims),
        out_shape=jax.ShapeDtypeStruct((n, r, width), F32),
        in_specs=[smem, smem, vmem, vmem, vmem, vmem], out_specs=vmem,
        scratch_shapes=[
            pltpu.VMEM((block * pairs, points), BF16),
            pltpu.VMEM((kcount, pairs, nrows), F32),
            pltpu.VMEM((kcount, pairs, points), F32),
            pltpu.VMEM((kcount, nval * ntrial, points), F32),
            pltpu.VMEM((nval * ntrial, nrows + points), BF16),
            pltpu.VMEM((nwa, nval * ntrial, width), F32),
        ],
        name="compute",
    )(row, inverse, val, cond, tri, weights)
    mine = pl.pallas_call(
        functools.partial(reduce_kernel, npb, nwa),
        out_shape=jax.ShapeDtypeStruct((r, width), F32),
        in_specs=[vmem], out_specs=vmem,
        scratch_shapes=[pltpu.VMEM((n, r, width), F32), pltpu.SemaphoreType.DMA] + [pltpu.SemaphoreType.DMA((n,))] * 2,
        compiler_params=pltpu.CompilerParams(collective_id=1, has_side_effects=True),
        name="reduce",
    )(partial)
    mine = mine.reshape(r, klocal, crows)[:, :, :ncond]
    return mine.transpose(1, 0, 2).reshape(klocal, cols)


def solution(mesh):
    in_specs = (
        P("wa", None, "pb"),
        P("wa", None, "pb"),
        P("wa", "pb"),
        P("pb", "wa", None),
        P("pb", None),
    )
    body = functools.partial(shards, mesh.shape["pb"], mesh.shape["wa"])
    return jax.shard_map(body, mesh=mesh, in_specs=in_specs, out_specs=P("wa", "pb"), check_vma=False)
```

time: 309 us -> 67.9 us (0.22)
  the two profiles are of different devices: /device:TPU:5 before, /device:TPU:0 now
where the time goes in v1:
time: 67.9 us; the launch traced here: 67.5 us
  Pallas kernels  50.2 us (74%)
  local copies, waits for them, and re-layouts  15 us (22%)
  other arithmetic  2.06 us (3%)
    pallas_call x1, Pallas kernels, shards(): pl.pallas_call(functools.partial(compute_kernel, dims), out_shape=jax.Sha...  21.1 us
    pallas_call x1, Pallas kernels, shards(): pl.pallas_call(functools.partial(gather_kernel, npb, nwa), out_shape=jax....  16.5 us
    pallas_call x1, Pallas kernels, shards(): pl.pallas_call(functools.partial(reduce_kernel, npb, nwa), out_shape=jax....  12.7 us
    convert_element_type x3, local copies, waits for them, and re-layouts, shards(): val.transpose(1, 3, 4, 0, 2, 5).reshape(kcount, nval, points).astype(F32)  2.95 us
    reshape x1, local copies, waits for them, and re-layouts, shards(): gathered = gathered.reshape(npb // 2, nwa, 2, rows * LANES)  2.11 us
    reshape x2, local copies, waits for them, and re-layouts, shards(): cond = cond.transpose(1, 3, 4, 0, 2, 5).reshape(kcount, ncond, points)  1.37 us

profile of v1, /device:TPU:0, one launch (start us, length us, event | category | flops | bytes accessed | tf_op | source)
XLA Modules:
  0.0 67.5 jit_solution(2413684822622538430)
XLA Ops:
  0.0 0.0 copy-start.1
  0.0 1.3 %select_reduce_fusion.inv_ref = s32[16]{0:T(128)} fusion(s32[16]{0:T(128)} %bitcast.31), kind=kLoop, calls=%fused_computation.9 | loop fusion | flops 752 | bytes 128 | tf_op jit(solution)/shard_map/reduce_sum | solution.py:221
  1.3 0.8 %reshape.44 = bf16[768]{0:T(1024)(128)(2,1)S(1)} reshape(bf16[8,96]{1,0:T(8,128)(2,1)} %param.7) | data formatting | bytes 3072 | tf_op jit(solution)/shard_map/reshape | solution.py:227
  2.1 0.8 %reshape.42 = bf16[4096]{0:T(1024)(128)(2,1)S(1)} reshape(bf16[8,8,64]{2,1,0:T(8,128)(2,1)} %param.5) | data formatting | bytes 16384 | tf_op jit(solution)/shard_map/reshape | solution.py:227
  2.9 0.0 copy-done.1
  2.9 0.1 reshape.43
  3.0 0.6 fusion.5.x_ref
  3.6 16.5 %gather.1 = bf16[32,96,128]{2,1,0:T(8,128)(2,1)} custom-call(bf16[96,128]{1,0:T(8,128)(2,1)} %fusion.5.x_ref), custom_call_target="tpu_custom_call" | custom-call | tf_op jit(solution)/shard_map/gather/pallas_call | solution.py:233
  20.1 2.1 %reshape.46 = bf16[8,2,2,12288]{3,2,1,0:T(2,128)(2,1)S(1)} reshape(bf16[32,96,128]{2,1,0:T(8,128)(2,1)} %gather.1) | data formatting | bytes 1572864 | tf_op jit(solution)/shard_map/reshape | solution.py:241
  22.2 0.0 copy-start
  22.3 0.1 reshape.49
  22.4 0.7 copy-done
  23.1 0.3 slice.17
  23.3 0.0 slice-start
  23.3 0.2 copy.28
  23.6 0.7 %slice-done = bf16[8,2,2,4096]{3,2,1,0:T(2,128)(2,1)S(1)} async-done(((bf16[8,2,2,12288]{3,2,1,0:T(2,128)(2,1)}), bf16[8,2,2,4096]{3,2,1,0:T(2,128)(2,1)S(1)}, s32[]{:S(2)}) %slice-start) | async-done | bytes 262168 | tf_op jit(solution)/shard_map/slice | solution.py:243
  24.3 0.2 copy_convert_fusion
  24.4 0.4 reshape.50
  24.8 0.3 copy.23
  25.2 1.0 %pad.14.x_ref = bf16[16,128,16]{2,1,0:T(8,128)(2,1)} pad(bf16[16,128,12]{2,1,0:T(8,128)(2,1)S(1)} %bitcast.28, bf16[]{:T(256)} %constant.3.clone.1), padding=0_0x0_0x0_4 | pad | bytes 114690 | tf_op jit(solution)/shard_map/jit(_pad)/pad | solution.py:251
  26.1 0.4 reshape.55
  26.5 0.8 %copy.18 = f32[2,8,8,8,2,64]{5,4,3,2,1,0:T(2,128)S(1)} copy(f32[2,8,8,8,2,64]{5,2,1,3,4,0:T(8,128)S(1)} %bitcast.26) | data formatting | bytes 1048576 | tf_op jit(solution)/shard_map/convert_element_type | solution.py:246
  27.3 1.7 %reshape.54.val_ref = f32[16,8,1024]{2,1,0:T(8,128)} reshape(f32[2,8,8,8,2,64]{5,4,3,2,1,0:T(2,128)S(1)} %copy.18) | data formatting | bytes 1048576 | tf_op jit(solution)/shard_map/convert_element_type | solution.py:246
  29.1 0.9 %reshape.47 = bf16[8,2,2,8,12,64]{5,4,3,0,2,1:T(8,128)(2,1)S(1)} reshape(bf16[8,2,2,6144]{3,0,2,1:T(8,128)(2,1)S(1)} %copy.28) | data formatting | bytes 786432 | tf_op jit(solution)/shard_map/reshape | solution.py:244
  30.0 0.8 %copy.25 = bf16[2,8,12,8,2,64]{5,4,3,2,1,0:T(2,128)(2,1)S(1)} copy(bf16[2,8,12,8,2,64]{5,2,1,3,4,0:T(8,128)(2,1)S(1)} %bitcast.25) | data formatting | bytes 786432 | tf_op jit(solution)/shard_map/reshape | solution.py:247
  30.8 0.6 reshape.56
  31.4 0.9 %pad.13.cond_ref = bf16[16,16,1024]{2,1,0:T(8,128)(2,1)} pad(bf16[16,12,1024]{2,1,0:T(8,128)(2,1)S(1)} %reshape.56, bf16[]{:T(256)} %constant.3.clone.1), padding=0_0x0_4x0_0 | pad | bytes 917506 | tf_op jit(solution)/shard_map/jit(_pad)/pad | solution.py:249
  32.3 21.1 %compute.1.x_ref = f32[32,8,128]{2,1,0:T(8,128)} custom-call(s32[16]{0:T(128)} %bitcast.32, s32[16]{0:T(128)} %select_reduce_fusion.inv_ref, f32[16,8,1024]{2,1,0:T(8,128)} %reshape.54.val_ref, bf16[16,16,1024]{2,1,0:T(8,128)(2,1)} %pad.13.cond_ref, bf16[16,128,16]{2,1,0:T(8,128)(2,1)} %pad.14.x_ref, bf16[512,1024]{1,0:T(8,128)(2,1)} %bitcast.29), custom_call_target="tpu_custom_call" | custom-call | tf_op jit(solution)/shard_map/compute/pallas_call | solution.py:258
  53.4 12.7 %reduce.1 = f32[8,128]{1,0:T(8,128)} custom-call(f32[32,8,128]{2,1,0:T(8,128)} %compute.1.x_ref), custom_call_target="tpu_custom_call" | custom-call | tf_op jit(solution)/shard_map/reduce/pallas_call | solution.py:272
  66.0 0.7 %reshape.52 = f32[8,8,16]{2,1,0:T(8,128)S(1)} reshape(f32[8,128]{1,0:T(8,128)} %reduce.1) | data formatting | bytes 8192 | tf_op jit(solution)/shard_map/reshape | solution.py:280
  66.8 0.7 reshape.53
  (5 shorter events, 0.1 us)
Async XLA Ops:
  0.0 2.9 %copy-start.1 = (bf16[8,12,64]{2,0,1:T(8,128)(2,1)S(1)}, bf16[8,12,64]{2,0,1:T(8,128)(2,1)}, u32[]{:S(2)}) copy-start(bf16[8,12,64]{2,0,1:T(8,128)(2,1)} %param.6) | copy-start | bytes 36868
  22.2 0.9 %copy-start = (bf16[8,2,2,12288]{3,2,1,0:T(2,128)(2,1)}, bf16[8,2,2,12288]{3,2,1,0:T(2,128)(2,1)S(1)}, u32[]{:S(2)}) copy-start(bf16[8,2,2,12288]{3,2,1,0:T(2,128)(2,1)S(1)} %reshape.46) | copy-start | bytes 2359300
  23.3 1.0 %slice-start = ((bf16[8,2,2,12288]{3,2,1,0:T(2,128)(2,1)}), bf16[8,2,2,4096]{3,2,1,0:T(2,128)(2,1)S(1)}, s32[]{:S(2)}) async-start(bf16[8,2,2,12288]{3,2,1,0:T(2,128)(2,1)} %copy-done), calls=%async_computation | async-start | bytes 524288 | tf_op jit(solution)/shard_map/slice | solution.py:243

commit v2 on v1

v2 whole, which is shorter than its diff:
```python
import functools
import math

import jax
import jax.numpy as jnp
from jax import lax
from jax.experimental import pallas as pl
from jax.experimental.pallas import tpu as pltpu
from jax.sharding import PartitionSpec as P

MESH = pl.DeviceIdType.MESH
LANES = 128
PACK = 16
F32 = jnp.float32
BF16 = jnp.bfloat16


def up(value, unit):
    return -(-value // unit) * unit


def kernel(dims, kmap_ref, x_ref, w_ref, out_ref, slots, val_ref, cond_ref, condb_ref, tri_ref,
           a_ref, wa_ref, aw_ref, y_ref, z_ref, acc_ref, part_ref, rslots,
           own_sem, send_sem, recv_sem, fsend_sem, frecv_sem, rsend_sem, rrecv_sem):
    npb, nwa, klocal, nval, ncond, pts, ntrial, nrows, g, r = dims
    kcount, points, n = klocal * nwa, pts * npb, npb * nwa
    crows = condb_ref.shape[1]
    pb, wa = lax.axis_index("pb"), lax.axis_index("wa")
    me = wa * npb + pb
    nx = 2 if npb % 4 == 0 else 1
    nz = npb // (2 * nx)
    core, px, pz = lax.rem(pb, 2), lax.rem(pb // 2, nx), pb // (2 * nx)

    def device(z, x, y, c):
        return (z * nx + x) * 2 + c, y

    def source(z, x, y):
        return (lax.rem(pz - z + nz, nz), lax.rem(px - x + nx, nx), lax.rem(wa - y + nwa, nwa))

    def target(z, x, y):
        return (lax.rem(pz + z, nz), lax.rem(px + x, nx), lax.rem(wa + y, nwa))

    def slot(z, x, y, c):
        p, w = device(z, x, y, c)
        return slots.at[w * npb + p]

    barrier = pltpu.get_barrier_semaphore()

    def greet(j, carry):
        t = lax.rem(me + j, n)
        pl.semaphore_signal(barrier, inc=1, device_id=(lax.rem(t, npb), t // npb), device_id_type=MESH)
        return carry

    lax.fori_loop(1, n, greet, 0)
    own = pltpu.make_async_copy(x_ref, slots.at[me], own_sem)
    own.start()
    pl.semaphore_wait(barrier, n - 1)

    def hop(z, x, y, last):
        held = (z if last != 0 else 0, x if last != 1 else 0, y if last != 2 else 0)
        step = (z if last == 0 else 0, x if last == 1 else 0, y if last == 2 else 0)
        from_ref = x_ref if held == (0, 0, 0) else slot(*source(*held), core)
        index = (z * nx + x) * nwa + y
        return pltpu.make_async_remote_copy(
            src_ref=from_ref, dst_ref=slot(*source(*held), core), send_sem=send_sem.at[index],
            recv_sem=recv_sem.at[index], device_id=device(*target(*step), core), device_id_type=MESH)

    def across(z, x, y):
        from_ref = x_ref if (z, x, y) == (0, 0, 0) else slot(*source(z, x, y), core)
        index = (z * nx + x) * nwa + y
        return pltpu.make_async_remote_copy(
            src_ref=from_ref, dst_ref=slot(*source(z, x, y), core), send_sem=fsend_sem.at[index],
            recv_sem=frecv_sem.at[index], device_id=device(pz, px, wa, 1 - core), device_id_type=MESH)

    def last_axis(z, x, y):
        if x == 0 and y == 0:
            return 0
        if x == 0 or y == 0:
            return 1 if y == 0 else 2
        return 2 if z % 2 == 0 else 1

    def onward(z, x, y):
        sends = []
        if (z, x, y) == (0, 0, 0):
            sends += [(q, 0, 0) for q in range(1, nz)]
        if x == 0 and y == 0:
            sends += [(z, q, 0) for q in range(1, nx)] + [(z, 0, q) for q in range(1, nwa)]
        elif y == 0 and z % 2 == 0:
            sends += [(z, x, q) for q in range(1, nwa)]
        elif x == 0 and z % 2 == 1:
            sends += [(z, q, y) for q in range(1, nx)]
        for place in sends:
            hop(*place, last_axis(*place)).start()
        across(z, x, y).start()

    places = [(z, x, y) for z in range(nz) for x in range(nx) for y in range(nwa)]
    places.sort(key=lambda place: (min(place[0], nz - place[0]) + place[1] + place[2], place))
    for place in places:
        if place != (0, 0, 0):
            hop(*place, last_axis(*place)).wait_recv()
        onward(*place)

    cond_ref[...] = jnp.zeros_like(cond_ref)
    row0 = pl.multiple_of(wa * nrows, nrows)
    own.wait()
    for place in places:
        across(*place).wait_recv()

    kk_count = klocal // g
    per = LANES // pts
    kpad = tri_ref.shape[0] // n
    lane_group = lax.broadcasted_iota(jnp.int32, (slots.shape[1], LANES), 1) // pts

    def unpack(t, carry):
        w, tile = t // (npb // per), lax.rem(t, npb // per)
        blocks = [slots[t * per + i].astype(F32) for i in range(per)]
        at = pl.ds(pl.multiple_of(tile * LANES, LANES), LANES)
        for i in range(per):
            base = kk_count * (nval + ncond)
            tri_ref[pl.ds((t * per + i) * kpad, klocal), :] = blocks[i][base:base + klocal]
        for j in range(g):
            whole = None
            for i in range(per):
                shift = (i - j) * pts % LANES
                moved = pltpu.roll(blocks[i], shift, 1) if shift else blocks[i]
                whole = moved if whole is None else jnp.where(lane_group == i, moved, whole)
            for kk in range(kk_count):
                k = w * klocal + j * kk_count + kk
                val_ref[k, :, at] = whole[kk * nval:(kk + 1) * nval]
                base = kk_count * nval + kk * ncond
                cond_ref[k, 0:ncond, at] = whole[base:base + ncond]
        return carry

    lax.fori_loop(0, n // per, unpack, 0)
    condb_ref[...] = cond_ref[...].astype(BF16)

    def inverse(k):
        found = jnp.int32(0)
        for j in range(kcount):
            found = jnp.where(kmap_ref[j] == k, j, found)
        return found

    pairs = nval * nval
    block = math.gcd(kcount, max(1, 256 // pairs))
    spread = nval // r

    def one_y(k, carry):
        w, kl = k // klocal, lax.rem(k, klocal)
        rows = {}
        parts = []
        for u in range(nval):
            if u // r not in rows:
                start = (w * npb + u // r) * kpad + kl
                rows[u // r] = tri_ref[pl.ds(start, ntrial, stride=spread * kpad), :]
            shift = -(u % r) * ncond % LANES
            parts.append((pltpu.roll(rows[u // r], shift, 1) if shift else rows[u // r])[:, :crows])
        left = jnp.concatenate(parts, axis=0).astype(BF16)
        y_ref[k] = lax.dot_general(left, condb_ref[k], (((1,), (0,)), ((), ())), preferred_element_type=F32)
        return carry

    lax.fori_loop(0, kcount, one_y, 0)

    def build(b, pick, start, width):
        for i in range(block):
            k = b * block + i
            here = val_ref[k, :, pl.ds(start, width)]
            there = val_ref[pick(k), :, pl.ds(start, width)]
            for v in range(0, nval, 2):
                two = jnp.concatenate([here[v:v + 1] * there, here[v + 1:v + 2] * there], axis=0)
                a_ref[i * pairs + v * nval:i * pairs + (v + 2) * nval, 0:width] = two.astype(BF16)

    def first(b, carry):
        build(b, lambda k: kmap_ref[k], 0, points)
        out = lax.dot_general(a_ref[...], w_ref[...], (((1,), (1,)), ((), ())), preferred_element_type=F32)
        wa_ref[pl.ds(b * block, block)] = out.astype(BF16).astype(F32).reshape(block, pairs, nrows)
        return carry

    lax.fori_loop(0, kcount // block, first, 0)

    def second(b, carry):
        build(b, inverse, row0, nrows)
        out = lax.dot_general(a_ref[:, 0:nrows], w_ref[...], (((1,), (0,)), ((), ())), preferred_element_type=F32)
        aw_ref[pl.ds(b * block, block)] = out.reshape(block, pairs, points)
        return carry

    lax.fori_loop(0, kcount // block, second, 0)
    acc_ref[...] = jnp.zeros_like(acc_ref)
    chunk = math.gcd(nrows, LANES)

    def combine(k, weight_ref, other, start, base, width):
        for c in range(0, width, chunk):
            at = pl.ds(pl.multiple_of(start + c, chunk), chunk)
            ys = [y_ref[other, u * ntrial:(u + 1) * ntrial, at] for u in range(nval)]
            for v in range(nval):
                total = None
                for u in range(nval):
                    row = v * nval + u
                    term = weight_ref[k, row:row + 1, c:c + chunk] * ys[u]
                    total = term if total is None else total + term
                z_ref[v * ntrial:(v + 1) * ntrial, base + c:base + c + chunk] = total.astype(BF16)

    def one_k(k, carry):
        combine(k, wa_ref, kmap_ref[k], row0, 0, nrows)
        combine(k, aw_ref, inverse(k), 0, nrows, points)
        spot = lax.rem(k, klocal)
        both = jnp.concatenate([condb_ref[k, :, pl.ds(row0, nrows)], condb_ref[k]], axis=1)
        wide = jnp.concatenate(
            [both * jnp.where(spot == j, 1.0, 0.0).astype(BF16) for j in range(klocal)], axis=0)
        acc_ref[k // klocal] += lax.dot_general(
            z_ref[...], wide, (((1,), (1,)), ((), ())), preferred_element_type=F32)
        return carry

    def give(w, i):
        return pltpu.make_async_remote_copy(
            src_ref=part_ref.at[w * npb + i], dst_ref=rslots.at[me], send_sem=rsend_sem.at[w * npb + i],
            recv_sem=rrecv_sem.at[me], device_id=(i, w), device_id_type=MESH)

    for w in range(nwa):
        lax.fori_loop(w * klocal, (w + 1) * klocal, one_k, 0)
        for i in range(npb):
            s, v0 = i * r // nval, i * r % nval
            part_ref[w * npb + i] = acc_ref[w, pl.ds(v0 * ntrial + s, r, stride=ntrial), :]

        def send(i, carry, w=w):
            to = lax.rem(pb + i, npb)

            @pl.when(jnp.logical_or(to != pb, wa != w))
            def go():
                give(w, to).start()
            return carry

        lax.fori_loop(0, npb, send, 0)

    def receive(j, carry):
        t = lax.rem(me + j, n)
        pltpu.make_async_remote_copy(
            src_ref=part_ref.at[t], dst_ref=rslots.at[t], send_sem=rsend_sem.at[t],
            recv_sem=rrecv_sem.at[t], device_id=(lax.rem(t, npb), t // npb), device_id_type=MESH).wait_recv()
        return carry

    lax.fori_loop(1, n, receive, 0)
    total = part_ref[me]

    def add(j, total):
        return total + rslots[lax.rem(me + j, n)]

    out_ref[...] = lax.fori_loop(1, n, add, total)

    def finish(j, carry):
        t = lax.rem(me + j, n)
        give(t // npb, lax.rem(t, npb)).wait_send()
        return carry

    lax.fori_loop(1, n, finish, 0)
    for place in places:
        if place != (0, 0, 0):
            hop(*place, last_axis(*place)).wait_send()
        across(*place).wait_send()


def shards(npb, nwa, psi_val, psi_cond, trials, screened, kmap):
    klocal, nval, pts = psi_val.shape
    ncond = psi_cond.shape[1]
    cols = trials.shape[1]
    kcount, points, n = klocal * nwa, pts * npb, npb * nwa
    ntrial = cols * npb // (nval * ncond)
    weights = screened[0]
    nrows = weights.shape[0]
    vmem = pl.BlockSpec(memory_space=pltpu.VMEM)
    smem = pl.BlockSpec(memory_space=pltpu.SMEM)
    g = math.gcd(klocal, LANES // pts)
    kk = klocal // g

    def lanes(a):
        a = a.reshape(g, kk * a.shape[1], pts)
        a = jnp.concatenate([a[j] for j in range(g)], axis=1)
        return jnp.pad(a, ((0, 0), (0, LANES - a.shape[1])))

    rows = kk * (nval + ncond) + klocal
    prow = up(rows, PACK)
    packed = jnp.concatenate(
        [lanes(psi_val), lanes(psi_cond), jnp.pad(trials, ((0, prow - rows), (0, LANES - cols)))], axis=0)
    r = cols // ncond
    crows = up(ncond, PACK)
    width = klocal * crows
    pairs = nval * nval
    block = math.gcd(kcount, max(1, 256 // pairs))
    dims = (npb, nwa, klocal, nval, ncond, pts, ntrial, nrows, g, r)
    dma = pltpu.SemaphoreType.DMA
    mine = pl.pallas_call(
        functools.partial(kernel, dims),
        out_shape=jax.ShapeDtypeStruct((r, width), F32),
        in_specs=[smem, vmem, vmem], out_specs=vmem,
        scratch_shapes=[
            pltpu.VMEM((n, prow, LANES), BF16),
            pltpu.VMEM((kcount, nval, points), F32),
            pltpu.VMEM((kcount, crows, points), F32),
            pltpu.VMEM((kcount, crows, points), BF16),
            pltpu.VMEM((n * up(klocal, 8), LANES), F32),
            pltpu.VMEM((block * pairs, points), BF16),
            pltpu.VMEM((kcount, pairs, nrows), F32),
            pltpu.VMEM((kcount, pairs, points), F32),
            pltpu.VMEM((kcount, nval * ntrial, points), F32),
            pltpu.VMEM((nval * ntrial, nrows + points), BF16),
            pltpu.VMEM((nwa, nval * ntrial, width), F32),
            pltpu.VMEM((n, r, width), F32),
            pltpu.VMEM((n, r, width), F32),
            dma, dma((n // 2,)), dma((n // 2,)), dma((n // 2,)), dma((n // 2,)), dma((n,)), dma((n,)),
        ],
        compiler_params=pltpu.CompilerParams(collective_id=0, has_side_effects=True),
        name="bethe",
    )(kmap[0], packed, weights)
    mine = mine.reshape(r, klocal, crows)[:, :, :ncond]
    return mine.transpose(1, 0, 2).reshape(klocal, cols)


def solution(mesh):
    in_specs = (
        P("wa", None, "pb"),
        P("wa", None, "pb"),
        P("wa", "pb"),
        P("pb", "wa", None),
        P("pb", None),
    )
    body = functools.partial(shards, mesh.shape["pb"], mesh.shape["wa"])
    return jax.shard_map(body, mesh=mesh, in_specs=in_specs, out_specs=P("wa", "pb"), check_vma=False)
```

time: 67.9 us -> 51.2 us (0.75)
  the two profiles are of different devices: /device:TPU:0 before, /device:TPU:5 now
where the time goes in v2:
time: 51.2 us; the launch traced here: 51 us
  Pallas kernels  47.3 us (92%)
  local copies, waits for them, and re-layouts  2.92 us (6%)
  other arithmetic  0.68 us (1%)
    pallas_call x1, Pallas kernels, shards(): pl.pallas_call(functools.partial(kernel, dims), out_shape=jax.ShapeDtypeS...  47.3 us

profile of v2, /device:TPU:5, one launch (start us, length us, event | category | flops | bytes accessed | tf_op | source)
XLA Modules:
  0.0 51.0 jit_solution(13658120747208724935)
XLA Ops:
  0.0 0.0 copy-start
  0.0 0.7 %slice_bitcast_fusion.2 = (bf16[32,64]{1,0:T(8,128)(2,1)S(1)}, bf16[32,64]{1,0:T(8,128)(2,1)S(1)}) fusion(bf16[8,8,64]{2,1,0:T(8,128)(2,1)} %param.5), kind=kLoop, calls=%fused_computation.5 | loop fusion | bytes 16384 | tf_op jit(solution)/shard_map/squeeze | solution.py:276
  0.7 0.0 copy-done
  0.8 0.0 copy-start.1
  0.9 0.7 %copy-done.1 = bf16[8,96]{1,0:T(8,128)(2,1)S(1)} copy-done((bf16[8,96]{1,0:T(8,128)(2,1)S(1)}, bf16[8,96]{1,0:T(8,128)(2,1)}, u32[]{:S(2)}) %copy-start.1) | copy-done | bytes 1560
  1.5 0.7 %fusion.1.x_ref = bf16[96,128]{1,0:T(8,128)(2,1)} fusion(bf16[8,96]{1,0:T(8,128)(2,1)S(1)} %copy-done.1, bf16[48,64]{1,0:T(8,128)(2,1)S(1)} %squeeze.22, bf16[48,64]{1,0:T(8,128)(2,1)S(1)} %squeeze.21, bf16[32,64]{1,0:T(8,128)(2,1)S(1)} %get-tuple-element.8, bf16[32,64]{1,0:T(8,128)(2,1)S(1)} %get-tuple-element.7), kind=kLoop, calls=%fused_computation.3 | loop fusion | flops 147456 | bytes 46592 | tf_op jit(solution)/shard_map/concatenate | solution.py:281
  2.2 47.3 %bethe.1 = f32[8,128]{1,0:T(8,128)} custom-call(s32[16]{0:T(128)} %bitcast.9, bf16[96,128]{1,0:T(8,128)(2,1)} %fusion.1.x_ref, bf16[512,1024]{1,0:T(8,128)(2,1)} %bitcast.8), custom_call_target="tpu_custom_call" | custom-call | tf_op jit(solution)/shard_map/bethe/pallas_call | solution.py:290
  49.5 0.8 %reshape.16 = f32[8,8,16]{2,1,0:T(8,128)S(1)} reshape(f32[8,128]{1,0:T(8,128)} %bethe.1) | data formatting | bytes 8192 | tf_op jit(solution)/shard_map/reshape | solution.py:313
  50.3 0.7 %reshape.17 = f32[8,96]{1,0:T(8,128)} reshape(f32[8,8,12]{2,1,0:T(8,128)S(1)} %copy.11) | data formatting | bytes 6144 | tf_op jit(solution)/shard_map/reshape | solution.py:314
  (7 shorter events, 0.1 us)
Async XLA Ops:
  0.0 0.8 %copy-start = (bf16[8,12,64]{2,0,1:T(8,128)(2,1)S(1)}, bf16[8,12,64]{2,0,1:T(8,128)(2,1)}, u32[]{:S(2)}) copy-start(bf16[8,12,64]{2,0,1:T(8,128)(2,1)} %param.6) | copy-start | bytes 36868
  0.8 0.7 %copy-start.1 = (bf16[8,96]{1,0:T(8,128)(2,1)S(1)}, bf16[8,96]{1,0:T(8,128)(2,1)}, u32[]{:S(2)}) copy-start(bf16[8,96]{1,0:T(8,128)(2,1)} %param.7) | copy-start | bytes 4612

commit v3 on v2

--- a/solution.py
+++ b/solution.py
@@ -158,36 +158,42 @@
         y_ref[k] = lax.dot_general(left, condb_ref[k], (((1,), (0,)), ((), ())), preferred_element_type=F32)
         return carry
 
-    lax.fori_loop(0, kcount, one_y, 0)
-
-    def build(b, pick, start, width):
+    lax.fori_loop(0, kcount, one_y, 0, unroll=math.gcd(kcount, 4))
+
+    def build(half, b, pick, start, width):
         for i in range(block):
             k = b * block + i
             here = val_ref[k, :, pl.ds(start, width)]
             there = val_ref[pick(k), :, pl.ds(start, width)]
             for v in range(0, nval, 2):
                 two = jnp.concatenate([here[v:v + 1] * there, here[v + 1:v + 2] * there], axis=0)
-                a_ref[i * pairs + v * nval:i * pairs + (v + 2) * nval, 0:width] = two.astype(BF16)
-
-    def first(b, carry):
-        build(b, lambda k: kmap_ref[k], 0, points)
-        out = lax.dot_general(a_ref[...], w_ref[...], (((1,), (1,)), ((), ())), preferred_element_type=F32)
-        wa_ref[pl.ds(b * block, block)] = out.astype(BF16).astype(F32).reshape(block, pairs, nrows)
-        return carry
-
-    lax.fori_loop(0, kcount // block, first, 0)
-
-    def second(b, carry):
-        build(b, inverse, row0, nrows)
-        out = lax.dot_general(a_ref[:, 0:nrows], w_ref[...], (((1,), (0,)), ((), ())), preferred_element_type=F32)
-        aw_ref[pl.ds(b * block, block)] = out.reshape(block, pairs, points)
-        return carry
-
-    lax.fori_loop(0, kcount // block, second, 0)
+                a_ref[half, i * pairs + v * nval:i * pairs + (v + 2) * nval, 0:width] = two.astype(BF16)
+
+    def first(step, carry):
+        for half in range(halves):
+            b = step * halves + half
+            build(half, b, lambda k: kmap_ref[k], 0, points)
+            out = lax.dot_general(a_ref[half], w_ref[...], (((1,), (1,)), ((), ())), preferred_element_type=F32)
+            wa_ref[pl.ds(b * block, block)] = out.astype(BF16).astype(F32).reshape(block, pairs, nrows)
+        return carry
+
+    halves = a_ref.shape[0]
+    lax.fori_loop(0, kcount // block // halves, first, 0)
+
+    def second(step, carry):
+        for half in range(halves):
+            b = step * halves + half
+            build(half, b, inverse, row0, nrows)
+            out = lax.dot_general(a_ref[half, :, 0:nrows], w_ref[...], (((1,), (0,)), ((), ())), preferred_element_type=F32)
+            aw_ref[pl.ds(b * block, block)] = out.reshape(block, pairs, points)
+        return carry
+
+    lax.fori_loop(0, kcount // block // halves, second, 0)
     acc_ref[...] = jnp.zeros_like(acc_ref)
     chunk = math.gcd(nrows, LANES)
-
-    def combine(k, weight_ref, other, start, base, width):
+    group = z_ref.shape[0]
+
+    def combine(i, k, weight_ref, other, start, base, width):
         for c in range(0, width, chunk):
             at = pl.ds(pl.multiple_of(start + c, chunk), chunk)
             ys = [y_ref[other, u * ntrial:(u + 1) * ntrial, at] for u in range(nval)]
@@ -197,17 +203,21 @@
                     row = v * nval + u
                     term = weight_ref[k, row:row + 1, c:c + chunk] * ys[u]
                     total = term if total is None else total + term
-                z_ref[v * ntrial:(v + 1) * ntrial, base + c:base + c + chunk] = total.astype(BF16)
-
-    def one_k(k, carry):
-        combine(k, wa_ref, kmap_ref[k], row0, 0, nrows)
-        combine(k, aw_ref, inverse(k), 0, nrows, points)
-        spot = lax.rem(k, klocal)
-        both = jnp.concatenate([condb_ref[k, :, pl.ds(row0, nrows)], condb_ref[k]], axis=1)
-        wide = jnp.concatenate(
-            [both * jnp.where(spot == j, 1.0, 0.0).astype(BF16) for j in range(klocal)], axis=0)
-        acc_ref[k // klocal] += lax.dot_general(
-            z_ref[...], wide, (((1,), (1,)), ((), ())), preferred_element_type=F32)
+                z_ref[i, v * ntrial:(v + 1) * ntrial, base + c:base + c + chunk] = total.astype(BF16)
+
+    def some_k(step, carry):
+        total = None
+        for i in range(group):
+            k = step * group + i
+            combine(i, k, wa_ref, kmap_ref[k], row0, 0, nrows)
+            combine(i, k, aw_ref, inverse(k), 0, nrows, points)
+            spot = lax.rem(k, klocal)
+            both = jnp.concatenate([condb_ref[k, :, pl.ds(row0, nrows)], condb_ref[k]], axis=1)
+            wide = jnp.concatenate(
+                [both * jnp.where(spot == j, 1.0, 0.0).astype(BF16) for j in range(klocal)], axis=0)
+            term = lax.dot_general(z_ref[i], wide, (((1,), (1,)), ((), ())), preferred_element_type=F32)
+            total = term if total is None else total + term
+        acc_ref[step * group // klocal] += total
         return carry
 
     def give(w, i):
@@ -216,7 +226,7 @@
             recv_sem=rrecv_sem.at[me], device_id=(i, w), device_id_type=MESH)
 
     for w in range(nwa):
-        lax.fori_loop(w * klocal, (w + 1) * klocal, one_k, 0)
+        lax.fori_loop(w * klocal // group, (w + 1) * klocal // group, some_k, 0)
         for i in range(npb):
             s, v0 = i * r // nval, i * r % nval
             part_ref[w * npb + i] = acc_ref[w, pl.ds(v0 * ntrial + s, r, stride=ntrial), :]
@@ -297,11 +307,11 @@
             pltpu.VMEM((kcount, crows, points), F32),
             pltpu.VMEM((kcount, crows, points), BF16),
             pltpu.VMEM((n * up(klocal, 8), LANES), F32),
-            pltpu.VMEM((block * pairs, points), BF16),
+            pltpu.VMEM((math.gcd(kcount // block, 2), block * pairs, points), BF16),
             pltpu.VMEM((kcount, pairs, nrows), F32),
             pltpu.VMEM((kcount, pairs, points), F32),
             pltpu.VMEM((kcount, nval * ntrial, points), F32),
-            pltpu.VMEM((nval * ntrial, nrows + points), BF16),
+            pltpu.VMEM((math.gcd(klocal, 4), nval * ntrial, nrows + points), BF16),
             pltpu.VMEM((nwa, nval * ntrial, width), F32),
             pltpu.VMEM((n, r, width), F32),
             pltpu.VMEM((n, r, width), F32),

time: 51.2 us -> 46.9 us (0.916)
  Pallas kernels: 47.3 us -> 43 us
    pallas_call x1, Pallas kernels: 47.3 us -> 43 us  [shards(): pl.pallas_call(functools.partial(kernel, dims), out_shape=jax.ShapeDtypeS...]
where the time goes in v3:
time: 46.9 us; the launch traced here: 46.7 us
  Pallas kernels  43 us (92%)
  local copies, waits for them, and re-layouts  2.92 us (6%)
  other arithmetic  0.68 us (1%)
    pallas_call x1, Pallas kernels, shards(): pl.pallas_call(functools.partial(kernel, dims), out_shape=jax.ShapeDtypeS...  43 us

profile of v3, /device:TPU:5, one launch (start us, length us, event | category | flops | bytes accessed | tf_op | source)
XLA Modules:
  0.0 46.7 jit_solution(16223224444105594969)
XLA Ops:
  0.0 0.0 copy-start
  0.0 0.7 %slice_bitcast_fusion.2 = (bf16[32,64]{1,0:T(8,128)(2,1)S(1)}, bf16[32,64]{1,0:T(8,128)(2,1)S(1)}) fusion(bf16[8,8,64]{2,1,0:T(8,128)(2,1)} %param.5), kind=kLoop, calls=%fused_computation.5 | loop fusion | bytes 16384 | tf_op jit(solution)/shard_map/squeeze | solution.py:286
  0.7 0.0 copy-done
  0.8 0.0 copy-start.1
  0.9 0.7 %copy-done.1 = bf16[8,96]{1,0:T(8,128)(2,1)S(1)} copy-done((bf16[8,96]{1,0:T(8,128)(2,1)S(1)}, bf16[8,96]{1,0:T(8,128)(2,1)}, u32[]{:S(2)}) %copy-start.1) | copy-done | bytes 1560
  1.5 0.7 %fusion.1.x_ref = bf16[96,128]{1,0:T(8,128)(2,1)} fusion(bf16[8,96]{1,0:T(8,128)(2,1)S(1)} %copy-done.1, bf16[48,64]{1,0:T(8,128)(2,1)S(1)} %squeeze.22, bf16[48,64]{1,0:T(8,128)(2,1)S(1)} %squeeze.21, bf16[32,64]{1,0:T(8,128)(2,1)S(1)} %get-tuple-element.8, bf16[32,64]{1,0:T(8,128)(2,1)S(1)} %get-tuple-element.7), kind=kLoop, calls=%fused_computation.3 | loop fusion | flops 147456 | bytes 46592 | tf_op jit(solution)/shard_map/concatenate | solution.py:291
  2.2 43.0 %bethe.1 = f32[8,128]{1,0:T(8,128)} custom-call(s32[16]{0:T(128)} %bitcast.9, bf16[96,128]{1,0:T(8,128)(2,1)} %fusion.1.x_ref, bf16[512,1024]{1,0:T(8,128)(2,1)} %bitcast.8), custom_call_target="tpu_custom_call" | custom-call | tf_op jit(solution)/shard_map/bethe/pallas_call | solution.py:300
  45.2 0.8 %reshape.16 = f32[8,8,16]{2,1,0:T(8,128)S(1)} reshape(f32[8,128]{1,0:T(8,128)} %bethe.1) | data formatting | bytes 8192 | tf_op jit(solution)/shard_map/reshape | solution.py:323
  46.0 0.7 %reshape.17 = f32[8,96]{1,0:T(8,128)} reshape(f32[8,8,12]{2,1,0:T(8,128)S(1)} %copy.11) | data formatting | bytes 6144 | tf_op jit(solution)/shard_map/reshape | solution.py:324
  (7 shorter events, 0.1 us)
Async XLA Ops:
  0.0 0.8 %copy-start = (bf16[8,12,64]{2,0,1:T(8,128)(2,1)S(1)}, bf16[8,12,64]{2,0,1:T(8,128)(2,1)}, u32[]{:S(2)}) copy-start(bf16[8,12,64]{2,0,1:T(8,128)(2,1)} %param.6) | copy-start | bytes 36868
  0.8 0.7 %copy-start.1 = (bf16[8,96]{1,0:T(8,128)(2,1)S(1)}, bf16[8,96]{1,0:T(8,128)(2,1)}, u32[]{:S(2)}) copy-start(bf16[8,96]{1,0:T(8,128)(2,1)} %param.7) | copy-start | bytes 4612

commit v4 on v3

--- a/solution.py
+++ b/solution.py
@@ -19,7 +19,7 @@
     return -(-value // unit) * unit
 
 
-def kernel(dims, kmap_ref, x_ref, w_ref, out_ref, slots, val_ref, cond_ref, condb_ref, tri_ref,
+def kernel(dims, kmap_ref, x_ref, whbm_ref, out_ref, w_ref, w_sem, slots, val_ref, cond_ref, condb_ref, tri_ref,
            a_ref, wa_ref, aw_ref, y_ref, z_ref, acc_ref, part_ref, rslots,
            own_sem, send_sem, recv_sem, fsend_sem, frecv_sem, rsend_sem, rrecv_sem):
     npb, nwa, klocal, nval, ncond, pts, ntrial, nrows, g, r = dims
@@ -54,6 +54,11 @@
     lax.fori_loop(1, n, greet, 0)
     own = pltpu.make_async_copy(x_ref, slots.at[me], own_sem)
     own.start()
+    load = pltpu.make_async_copy(whbm_ref.at[0], w_ref, w_sem)
+    load.start()
+    cond_ref[...] = jnp.zeros_like(cond_ref)
+    acc_ref[...] = jnp.zeros_like(acc_ref)
+    own.wait()
     pl.semaphore_wait(barrier, n - 1)
 
     def hop(z, x, y, last):
@@ -95,16 +100,7 @@
 
     places = [(z, x, y) for z in range(nz) for x in range(nx) for y in range(nwa)]
     places.sort(key=lambda place: (min(place[0], nz - place[0]) + place[1] + place[2], place))
-    for place in places:
-        if place != (0, 0, 0):
-            hop(*place, last_axis(*place)).wait_recv()
-        onward(*place)
-
-    cond_ref[...] = jnp.zeros_like(cond_ref)
     row0 = pl.multiple_of(wa * nrows, nrows)
-    own.wait()
-    for place in places:
-        across(*place).wait_recv()
 
     kk_count = klocal // g
     per = LANES // pts
@@ -131,7 +127,25 @@
                 cond_ref[k, 0:ncond, at] = whole[base:base + ncond]
         return carry
 
-    lax.fori_loop(0, n // per, unpack, 0)
+    early = per == 2
+    lag = 3
+
+    def collect(place):
+        across(*place).wait_recv()
+        if early:
+            z, x, y = source(*place)
+            unpack(y * (npb // 2) + z * nx + x, 0)
+
+    for number, place in enumerate(places):
+        if place != (0, 0, 0):
+            hop(*place, last_axis(*place)).wait_recv()
+        onward(*place)
+        if number >= lag:
+            collect(places[number - lag])
+    for place in places[-lag:] if len(places) >= lag else places:
+        collect(place)
+    if not early:
+        lax.fori_loop(0, n // per, unpack, 0)
     condb_ref[...] = cond_ref[...].astype(BF16)
 
     def inverse(k):
@@ -169,6 +183,8 @@
                 two = jnp.concatenate([here[v:v + 1] * there, here[v + 1:v + 2] * there], axis=0)
                 a_ref[half, i * pairs + v * nval:i * pairs + (v + 2) * nval, 0:width] = two.astype(BF16)
 
+    load.wait()
+
     def first(step, carry):
         for half in range(halves):
             b = step * halves + half
@@ -189,7 +205,6 @@
         return carry
 
     lax.fori_loop(0, kcount // block // halves, second, 0)
-    acc_ref[...] = jnp.zeros_like(acc_ref)
     chunk = math.gcd(nrows, LANES)
     group = z_ref.shape[0]
 
@@ -274,8 +289,7 @@
     cols = trials.shape[1]
     kcount, points, n = klocal * nwa, pts * npb, npb * nwa
     ntrial = cols * npb // (nval * ncond)
-    weights = screened[0]
-    nrows = weights.shape[0]
+    nrows = screened.shape[1]
     vmem = pl.BlockSpec(memory_space=pltpu.VMEM)
     smem = pl.BlockSpec(memory_space=pltpu.SMEM)
     g = math.gcd(klocal, LANES // pts)
@@ -300,8 +314,10 @@
     mine = pl.pallas_call(
         functools.partial(kernel, dims),
         out_shape=jax.ShapeDtypeStruct((r, width), F32),
-        in_specs=[smem, vmem, vmem], out_specs=vmem,
+        in_specs=[smem, vmem, pl.BlockSpec(memory_space=pl.ANY)], out_specs=vmem,
         scratch_shapes=[
+            pltpu.VMEM((nrows, points), BF16),
+            dma,
             pltpu.VMEM((n, prow, LANES), BF16),
             pltpu.VMEM((kcount, nval, points), F32),
             pltpu.VMEM((kcount, crows, points), F32),
@@ -319,7 +335,7 @@
         ],
         compiler_params=pltpu.CompilerParams(collective_id=0, has_side_effects=True),
         name="bethe",
-    )(kmap[0], packed, weights)
+    )(kmap[0], packed, screened)
     mine = mine.reshape(r, klocal, crows)[:, :, :ncond]
     return mine.transpose(1, 0, 2).reshape(klocal, cols)
 

time: 46.9 us -> 45.6 us (0.972)
  Pallas kernels: 43 us -> 41.6 us
    pallas_call x1, Pallas kernels: 43 us -> 41.6 us  [shards(): pl.pallas_call(functools.partial(kernel, dims), out_shape=jax.ShapeDtypeS...]
where the time goes in v4:
time: 45.6 us; the launch traced here: 45.3 us
  Pallas kernels  41.6 us (91%)
  local copies, waits for them, and re-layouts  2.92 us (6%)
  other arithmetic  0.68 us (1%)
    pallas_call x1, Pallas kernels, shards(): pl.pallas_call(functools.partial(kernel, dims), out_shape=jax.ShapeDtypeS...  41.6 us

profile of v4, /device:TPU:5, one launch (start us, length us, event | category | flops | bytes accessed | tf_op | source)
XLA Modules:
  0.0 45.3 jit_solution(10490496304006558738)
XLA Ops:
  0.0 0.0 copy-start
  0.0 0.7 %slice_bitcast_fusion.2 = (bf16[32,64]{1,0:T(8,128)(2,1)S(1)}, bf16[32,64]{1,0:T(8,128)(2,1)S(1)}) fusion(bf16[8,8,64]{2,1,0:T(8,128)(2,1)} %param.5), kind=kLoop, calls=%fused_computation.5 | loop fusion | bytes 16384 | tf_op jit(solution)/shard_map/squeeze | solution.py:300
  0.7 0.0 copy-done
  0.8 0.0 copy-start.1
  0.9 0.7 %copy-done.1 = bf16[8,96]{1,0:T(8,128)(2,1)S(1)} copy-done((bf16[8,96]{1,0:T(8,128)(2,1)S(1)}, bf16[8,96]{1,0:T(8,128)(2,1)}, u32[]{:S(2)}) %copy-start.1) | copy-done | bytes 1560
  1.5 0.7 %fusion.1.x_ref = bf16[96,128]{1,0:T(8,128)(2,1)} fusion(bf16[8,96]{1,0:T(8,128)(2,1)S(1)} %copy-done.1, bf16[48,64]{1,0:T(8,128)(2,1)S(1)} %squeeze.19, bf16[48,64]{1,0:T(8,128)(2,1)S(1)} %squeeze.18, bf16[32,64]{1,0:T(8,128)(2,1)S(1)} %get-tuple-element.8, bf16[32,64]{1,0:T(8,128)(2,1)S(1)} %get-tuple-element.7), kind=kLoop, calls=%fused_computation.3 | loop fusion | flops 147456 | bytes 46592 | tf_op jit(solution)/shard_map/concatenate | solution.py:305
  2.2 41.6 %bethe.1 = f32[8,128]{1,0:T(8,128)} custom-call(s32[16]{0:T(128)} %bitcast.7, bf16[96,128]{1,0:T(8,128)(2,1)} %fusion.1.x_ref, bf16[1,512,1024]{2,1,0:T(8,128)(2,1)} %whbm_ref.1), custom_call_target="tpu_custom_call" | custom-call | tf_op jit(solution)/shard_map/bethe/pallas_call | solution.py:314
  43.8 0.8 %reshape.16 = f32[8,8,16]{2,1,0:T(8,128)S(1)} reshape(f32[8,128]{1,0:T(8,128)} %bethe.1) | data formatting | bytes 8192 | tf_op jit(solution)/shard_map/reshape | solution.py:339
  44.6 0.7 %reshape.17 = f32[8,96]{1,0:T(8,128)} reshape(f32[8,8,12]{2,1,0:T(8,128)S(1)} %copy.11) | data formatting | bytes 6144 | tf_op jit(solution)/shard_map/reshape | solution.py:340
  (7 shorter events, 0.1 us)
Async XLA Ops:
  0.0 0.8 %copy-start = (bf16[8,12,64]{2,0,1:T(8,128)(2,1)S(1)}, bf16[8,12,64]{2,0,1:T(8,128)(2,1)}, u32[]{:S(2)}) copy-start(bf16[8,12,64]{2,0,1:T(8,128)(2,1)} %param.6) | copy-start | bytes 36868
  0.8 0.7 %copy-start.1 = (bf16[8,96]{1,0:T(8,128)(2,1)S(1)}, bf16[8,96]{1,0:T(8,128)(2,1)}, u32[]{:S(2)}) copy-start(bf16[8,96]{1,0:T(8,128)(2,1)} %param.7) | copy-start | bytes 4612
